TPU v7x, 32 devices: a whole 2x2x4 slice. The times are simulated.
32 devices in a mesh: space: 16 (over z, x, core), ens: 2 (over y).
Axes of the slice: x: 2, y: 2, z: 4, core: 2. Of those that a mesh axis runs over, the one named last changes fastest.
Arguments:
- params: float32 [64, 256, 512], P('ens', 'space'), may hold values from 0.55 to 0.8
- base_thickness: float32 [256, 512], P('space'), may hold values from 0.5 to 3
- balance: float32 [256, 512], P('space'), may hold values from -0.1 to 0.3
- step_count: int32 [64], replicated, may hold values from 8 to 32, as said below
- obs_index: int32 [4096], P('space'), may hold values from 0 to 8191
- observed: float32 [4096], P('space'), may hold values from 0.5 to 2
- noise_var: float32 [4096], P('space'), may hold values from 0.5 to 4
Outputs:
- thickness: float32 [64, 256, 512], P('ens', 'space')
- updated: float32 [64, 256, 512], P('ens', 'space')
Inputs may be any that keep to these rules, and one draw needn't show every extreme that they name: `step_count`: some member runs exactly 32 steps.
All inputs are finite; a program needn't handle non-finite values.
Results may differ from a plain program's by a relative error of at most 0.000074.
Values sent between devices are 32-bit elements; how exact they have to be, the bound alone decides.
A program may use at most 64 MiB of HBM per device.

v0:
```python
import jax
import jax.numpy as jnp
from jax import lax
from jax.sharding import PartitionSpec as P

time_step = 0.11


def padded_2(block, sides, width):
    for axis, dim in sides:
        count = lax.axis_size(axis)
        forward = [(i, i + 1) for i in range(count - 1)]
        backward = [(target, source) for source, target in forward]
        low = lax.ppermute(
            lax.slice_in_dim(block, block.shape[dim] - width, None, axis=dim), axis, forward
        )
        high = lax.ppermute(lax.slice_in_dim(block, 0, width, axis=dim), axis, backward)
        block = jnp.concatenate([low, block, high], axis=dim)
    return block


def stencil(padded, slip_padded, thickness, balance):
    diffusivity = slip_padded * padded * padded / (1.0 + padded * padded)
    centre = diffusivity[:, 1:-1, 1:-1]
    divergence = jnp.zeros_like(thickness)
    for row_part, col_part in (
        (slice(2, None), slice(1, -1)),
        (slice(None, -2), slice(1, -1)),
        (slice(1, -1), slice(2, None)),
        (slice(1, -1), slice(None, -2)),
    ):
        divergence = divergence + 0.5 * (diffusivity[:, row_part, col_part] + centre) * (
            padded[:, row_part, col_part] - thickness
        )
    return thickness + time_step * (divergence + balance)


def ensemble_terms(predicted, observed, noise_var):
    members = predicted.shape[0]
    scaling = lax.rsqrt(noise_var)
    average = jnp.mean(predicted, axis=0)
    anomalies = (predicted - average) * scaling / jnp.sqrt(jnp.float32(members - 1))
    mismatch = (observed - predicted) * scaling
    gram = jnp.dot(anomalies, anomalies.T, precision=lax.Precision.HIGHEST)
    cross = jnp.dot(anomalies, mismatch.T, precision=lax.Precision.HIGHEST)
    return (gram, cross)


def solve_weights(gram, cross):
    members = gram.shape[0]
    factor = jnp.linalg.cholesky(gram + jnp.eye(members, dtype=gram.dtype))
    inner = lax.linalg.triangular_solve(factor, cross, left_side=True, lower=True)
    result = lax.linalg.triangular_solve(
        factor, inner, left_side=True, lower=True, transpose_a=True
    )
    return result / jnp.sqrt(jnp.float32(members - 1))


def shards(params, base_thickness, balance, step_count, obs_index, observed, noise_var):
    members_dev = params.shape[0]
    ens_index = lax.axis_index("ens")
    members = members_dev * lax.axis_size("ens")
    own_counts = lax.dynamic_slice_in_dim(step_count, ens_index * members_dev, members_dev)
    longest = jnp.max(own_counts)
    initial = jnp.broadcast_to(base_thickness[None], params.shape)
    slip_rows = padded_2(jnp.exp(params), (("space", 1),), 1)
    slip_padded = jnp.pad(slip_rows, ((0, 0), (0, 0), (1, 1)))

    def advance(step_index, thickness):
        rimmed = padded_2(thickness, (("space", 1),), 1)
        padded = jnp.pad(rimmed, ((0, 0), (0, 0), (1, 1)))
        moved = stencil(padded, slip_padded, thickness, balance)
        return jnp.where((step_index < own_counts)[:, None, None], moved, thickness)

    thickness = lax.fori_loop(0, longest, advance, initial)
    tile_cells = params.shape[1] * params.shape[2]
    predicted = jnp.take(thickness.reshape(members_dev, tile_cells), obs_index, axis=1)
    obs_block = lax.all_to_all(predicted, "ens", split_axis=1, concat_axis=0, tiled=True)
    block_width = obs_block.shape[1]
    observed_part = lax.dynamic_slice_in_dim(observed, ens_index * block_width, block_width)
    noise_part = lax.dynamic_slice_in_dim(noise_var, ens_index * block_width, block_width)
    gram, cross = ensemble_terms(obs_block, observed_part, noise_part)
    gram, cross = lax.psum((gram, cross), ("space", "ens"))
    weights = solve_weights(gram, cross)
    weight_cols = lax.dynamic_slice_in_dim(weights, ens_index * members_dev, members_dev, 1)
    piece = lax.all_gather(params, "ens", axis=0, tiled=True)
    piece_rows = piece.shape[0]
    flat_piece = piece.reshape(piece_rows, tile_cells)
    weighted = jnp.dot(weight_cols.T, flat_piece, precision=lax.Precision.HIGHEST)
    weighted, member_total = (weighted, jnp.sum(flat_piece, axis=0))
    column_sums = jnp.sum(weight_cols, axis=0)
    increment = weighted - column_sums[:, None] * member_total[None, :] / members
    updated = params + increment.reshape(params.shape)
    return (thickness, updated)


def solution(mesh):
    in_specs = (
        P("ens", "space", None),
        P("space", None),
        P("space", None),
        P(),
        P("space"),
        P("space"),
        P("space"),
    )
    out_specs = (P("ens", "space", None), P("ens", "space", None))
    return jax.shard_map(shards, mesh=mesh, in_specs=in_specs, out_specs=out_specs, check_vma=False)
```

profile of v0, /device:TPU:0, one launch (start us, length us, event | category | flops | bytes accessed | tf_op | source)
XLA Modules:
  0.0 560.8 jit_solution(4297953380214112374)
XLA Ops:
  19.3 447.2 %while.12 = (s32[]{:T(128)}, f32[32,16,512]{2,1,0:T(8,128)}, s32[]{:T(128)}, s32[32]{0:T(128)S(1)}, f32[32,18,514]{2,1,0:T(8,128)S(1)}, /*index=5*/f32[16,512]{1,0:T(8,128)S(1)}, s32[]{:T(128)}) while((s32[]{:T(128)}, f32[32,16,512]{2,1,0:T(8,128)}, s32[]{:T(128)}, s32[32]{0:T(128)S(1)}, f32[32,18,514]{2,1,0:T(8,128)S(1)}, ...), condition=%wide.region_2.3_spmd, body=%wide.region_1.2_spmd.sunk | while | flops 10402466 | bytes 17217376 | solution.py:75
  22.6 5.4 collective-permute-start.1
  49.1 6.0 %collective-permute-start.1 = (f32[32,1,512]{2,1,0:T(1,128)S(1)}, f32[32,1,512]{2,1,0:T(1,128)S(1)}, u32[]{:S(2)}, u32[]{:S(2)}) collective-permute-start(f32[32,1,512]{2,1,0:T(1,128)S(1)} %get-tuple-element.150), channel_id=1, source_target_pairs={{0,2},{2,4},{4,6},{6,8},{8,10},{10,12},{12,14},{14,16},{16,18},{18... | collective-permute-start | bytes 196616 | tf_op jit(solution)/shard_map/while/body/ppermute | solution.py:14
  63.0 5.4 collective-permute-start.1
  76.4 6.0 %collective-permute-start.1 = (f32[32,1,512]{2,1,0:T(1,128)S(1)}, f32[32,1,512]{2,1,0:T(1,128)S(1)}, u32[]{:S(2)}, u32[]{:S(2)}) collective-permute-start(f32[32,1,512]{2,1,0:T(1,128)S(1)} %get-tuple-element.150), channel_id=1, source_target_pairs={{0,2},{2,4},{4,6},{6,8},{8,10},{10,12},{12,14},{14,16},{16,18},{18... | collective-permute-start | bytes 196616 | tf_op jit(solution)/shard_map/while/body/ppermute | solution.py:14
  90.3 6.0 %collective-permute-start.1 = (f32[32,1,512]{2,1,0:T(1,128)S(1)}, f32[32,1,512]{2,1,0:T(1,128)S(1)}, u32[]{:S(2)}, u32[]{:S(2)}) collective-permute-start(f32[32,1,512]{2,1,0:T(1,128)S(1)} %get-tuple-element.150), channel_id=1, source_target_pairs={{0,2},{2,4},{4,6},{6,8},{8,10},{10,12},{12,14},{14,16},{16,18},{18... | collective-permute-start | bytes 196616 | tf_op jit(solution)/shard_map/while/body/ppermute | solution.py:14
  130.8 5.3 collective-permute-start.1
  144.0 6.2 %collective-permute-start.1 = (f32[32,1,512]{2,1,0:T(1,128)S(1)}, f32[32,1,512]{2,1,0:T(1,128)S(1)}, u32[]{:S(2)}, u32[]{:S(2)}) collective-permute-start(f32[32,1,512]{2,1,0:T(1,128)S(1)} %get-tuple-element.150), channel_id=1, source_target_pairs={{0,2},{2,4},{4,6},{6,8},{8,10},{10,12},{12,14},{14,16},{16,18},{18... | collective-permute-start | bytes 196616 | tf_op jit(solution)/shard_map/while/body/ppermute | solution.py:14
  158.2 6.2 %collective-permute-start.1 = (f32[32,1,512]{2,1,0:T(1,128)S(1)}, f32[32,1,512]{2,1,0:T(1,128)S(1)}, u32[]{:S(2)}, u32[]{:S(2)}) collective-permute-start(f32[32,1,512]{2,1,0:T(1,128)S(1)} %get-tuple-element.150), channel_id=1, source_target_pairs={{0,2},{2,4},{4,6},{6,8},{8,10},{10,12},{12,14},{14,16},{16,18},{18... | collective-permute-start | bytes 196616 | tf_op jit(solution)/shard_map/while/body/ppermute | solution.py:14
  172.3 6.2 %collective-permute-start.1 = (f32[32,1,512]{2,1,0:T(1,128)S(1)}, f32[32,1,512]{2,1,0:T(1,128)S(1)}, u32[]{:S(2)}, u32[]{:S(2)}) collective-permute-start(f32[32,1,512]{2,1,0:T(1,128)S(1)} %get-tuple-element.150), channel_id=1, source_target_pairs={{0,2},{2,4},{4,6},{6,8},{8,10},{10,12},{12,14},{14,16},{16,18},{18... | collective-permute-start | bytes 196616 | tf_op jit(solution)/shard_map/while/body/ppermute | solution.py:14
  186.4 6.2 %collective-permute-start.1 = (f32[32,1,512]{2,1,0:T(1,128)S(1)}, f32[32,1,512]{2,1,0:T(1,128)S(1)}, u32[]{:S(2)}, u32[]{:S(2)}) collective-permute-start(f32[32,1,512]{2,1,0:T(1,128)S(1)} %get-tuple-element.150), channel_id=1, source_target_pairs={{0,2},{2,4},{4,6},{6,8},{8,10},{10,12},{12,14},{14,16},{16,18},{18... | collective-permute-start | bytes 196616 | tf_op jit(solution)/shard_map/while/body/ppermute | solution.py:14
  200.6 6.2 %collective-permute-start.1 = (f32[32,1,512]{2,1,0:T(1,128)S(1)}, f32[32,1,512]{2,1,0:T(1,128)S(1)}, u32[]{:S(2)}, u32[]{:S(2)}) collective-permute-start(f32[32,1,512]{2,1,0:T(1,128)S(1)} %get-tuple-element.150), channel_id=1, source_target_pairs={{0,2},{2,4},{4,6},{6,8},{8,10},{10,12},{12,14},{14,16},{16,18},{18... | collective-permute-start | bytes 196616 | tf_op jit(solution)/shard_map/while/body/ppermute | solution.py:14
  214.7 6.2 %collective-permute-start.1 = (f32[32,1,512]{2,1,0:T(1,128)S(1)}, f32[32,1,512]{2,1,0:T(1,128)S(1)}, u32[]{:S(2)}, u32[]{:S(2)}) collective-permute-start(f32[32,1,512]{2,1,0:T(1,128)S(1)} %get-tuple-element.150), channel_id=1, source_target_pairs={{0,2},{2,4},{4,6},{6,8},{8,10},{10,12},{12,14},{14,16},{16,18},{18... | collective-permute-start | bytes 196616 | tf_op jit(solution)/shard_map/while/body/ppermute | solution.py:14
  228.8 6.2 %collective-permute-start.1 = (f32[32,1,512]{2,1,0:T(1,128)S(1)}, f32[32,1,512]{2,1,0:T(1,128)S(1)}, u32[]{:S(2)}, u32[]{:S(2)}) collective-permute-start(f32[32,1,512]{2,1,0:T(1,128)S(1)} %get-tuple-element.150), channel_id=1, source_target_pairs={{0,2},{2,4},{4,6},{6,8},{8,10},{10,12},{12,14},{14,16},{16,18},{18... | collective-permute-start | bytes 196616 | tf_op jit(solution)/shard_map/while/body/ppermute | solution.py:14
  243.0 6.2 %collective-permute-start.1 = (f32[32,1,512]{2,1,0:T(1,128)S(1)}, f32[32,1,512]{2,1,0:T(1,128)S(1)}, u32[]{:S(2)}, u32[]{:S(2)}) collective-permute-start(f32[32,1,512]{2,1,0:T(1,128)S(1)} %get-tuple-element.150), channel_id=1, source_target_pairs={{0,2},{2,4},{4,6},{6,8},{8,10},{10,12},{12,14},{14,16},{16,18},{18... | collective-permute-start | bytes 196616 | tf_op jit(solution)/shard_map/while/body/ppermute | solution.py:14
  257.1 6.2 %collective-permute-start.1 = (f32[32,1,512]{2,1,0:T(1,128)S(1)}, f32[32,1,512]{2,1,0:T(1,128)S(1)}, u32[]{:S(2)}, u32[]{:S(2)}) collective-permute-start(f32[32,1,512]{2,1,0:T(1,128)S(1)} %get-tuple-element.150), channel_id=1, source_target_pairs={{0,2},{2,4},{4,6},{6,8},{8,10},{10,12},{12,14},{14,16},{16,18},{18... | collective-permute-start | bytes 196616 | tf_op jit(solution)/shard_map/while/body/ppermute | solution.py:14
  271.2 6.2 %collective-permute-start.1 = (f32[32,1,512]{2,1,0:T(1,128)S(1)}, f32[32,1,512]{2,1,0:T(1,128)S(1)}, u32[]{:S(2)}, u32[]{:S(2)}) collective-permute-start(f32[32,1,512]{2,1,0:T(1,128)S(1)} %get-tuple-element.150), channel_id=1, source_target_pairs={{0,2},{2,4},{4,6},{6,8},{8,10},{10,12},{12,14},{14,16},{16,18},{18... | collective-permute-start | bytes 196616 | tf_op jit(solution)/shard_map/while/body/ppermute | solution.py:14
  285.4 6.2 %collective-permute-start.1 = (f32[32,1,512]{2,1,0:T(1,128)S(1)}, f32[32,1,512]{2,1,0:T(1,128)S(1)}, u32[]{:S(2)}, u32[]{:S(2)}) collective-permute-start(f32[32,1,512]{2,1,0:T(1,128)S(1)} %get-tuple-element.150), channel_id=1, source_target_pairs={{0,2},{2,4},{4,6},{6,8},{8,10},{10,12},{12,14},{14,16},{16,18},{18... | collective-permute-start | bytes 196616 | tf_op jit(solution)/shard_map/while/body/ppermute | solution.py:14
  299.5 6.2 %collective-permute-start.1 = (f32[32,1,512]{2,1,0:T(1,128)S(1)}, f32[32,1,512]{2,1,0:T(1,128)S(1)}, u32[]{:S(2)}, u32[]{:S(2)}) collective-permute-start(f32[32,1,512]{2,1,0:T(1,128)S(1)} %get-tuple-element.150), channel_id=1, source_target_pairs={{0,2},{2,4},{4,6},{6,8},{8,10},{10,12},{12,14},{14,16},{16,18},{18... | collective-permute-start | bytes 196616 | tf_op jit(solution)/shard_map/while/body/ppermute | solution.py:14
  313.6 6.2 %collective-permute-start.1 = (f32[32,1,512]{2,1,0:T(1,128)S(1)}, f32[32,1,512]{2,1,0:T(1,128)S(1)}, u32[]{:S(2)}, u32[]{:S(2)}) collective-permute-start(f32[32,1,512]{2,1,0:T(1,128)S(1)} %get-tuple-element.150), channel_id=1, source_target_pairs={{0,2},{2,4},{4,6},{6,8},{8,10},{10,12},{12,14},{14,16},{16,18},{18... | collective-permute-start | bytes 196616 | tf_op jit(solution)/shard_map/while/body/ppermute | solution.py:14
  327.8 6.2 %collective-permute-start.1 = (f32[32,1,512]{2,1,0:T(1,128)S(1)}, f32[32,1,512]{2,1,0:T(1,128)S(1)}, u32[]{:S(2)}, u32[]{:S(2)}) collective-permute-start(f32[32,1,512]{2,1,0:T(1,128)S(1)} %get-tuple-element.150), channel_id=1, source_target_pairs={{0,2},{2,4},{4,6},{6,8},{8,10},{10,12},{12,14},{14,16},{16,18},{18... | collective-permute-start | bytes 196616 | tf_op jit(solution)/shard_map/while/body/ppermute | solution.py:14
  341.9 6.2 %collective-permute-start.1 = (f32[32,1,512]{2,1,0:T(1,128)S(1)}, f32[32,1,512]{2,1,0:T(1,128)S(1)}, u32[]{:S(2)}, u32[]{:S(2)}) collective-permute-start(f32[32,1,512]{2,1,0:T(1,128)S(1)} %get-tuple-element.150), channel_id=1, source_target_pairs={{0,2},{2,4},{4,6},{6,8},{8,10},{10,12},{12,14},{14,16},{16,18},{18... | collective-permute-start | bytes 196616 | tf_op jit(solution)/shard_map/while/body/ppermute | solution.py:14
  356.1 6.2 %collective-permute-start.1 = (f32[32,1,512]{2,1,0:T(1,128)S(1)}, f32[32,1,512]{2,1,0:T(1,128)S(1)}, u32[]{:S(2)}, u32[]{:S(2)}) collective-permute-start(f32[32,1,512]{2,1,0:T(1,128)S(1)} %get-tuple-element.150), channel_id=1, source_target_pairs={{0,2},{2,4},{4,6},{6,8},{8,10},{10,12},{12,14},{14,16},{16,18},{18... | collective-permute-start | bytes 196616 | tf_op jit(solution)/shard_map/while/body/ppermute | solution.py:14
  370.2 6.2 %collective-permute-start.1 = (f32[32,1,512]{2,1,0:T(1,128)S(1)}, f32[32,1,512]{2,1,0:T(1,128)S(1)}, u32[]{:S(2)}, u32[]{:S(2)}) collective-permute-start(f32[32,1,512]{2,1,0:T(1,128)S(1)} %get-tuple-element.150), channel_id=1, source_target_pairs={{0,2},{2,4},{4,6},{6,8},{8,10},{10,12},{12,14},{14,16},{16,18},{18... | collective-permute-start | bytes 196616 | tf_op jit(solution)/shard_map/while/body/ppermute | solution.py:14
  384.3 6.2 %collective-permute-start.1 = (f32[32,1,512]{2,1,0:T(1,128)S(1)}, f32[32,1,512]{2,1,0:T(1,128)S(1)}, u32[]{:S(2)}, u32[]{:S(2)}) collective-permute-start(f32[32,1,512]{2,1,0:T(1,128)S(1)} %get-tuple-element.150), channel_id=1, source_target_pairs={{0,2},{2,4},{4,6},{6,8},{8,10},{10,12},{12,14},{14,16},{16,18},{18... | collective-permute-start | bytes 196616 | tf_op jit(solution)/shard_map/while/body/ppermute | solution.py:14
  398.5 6.2 %collective-permute-start.1 = (f32[32,1,512]{2,1,0:T(1,128)S(1)}, f32[32,1,512]{2,1,0:T(1,128)S(1)}, u32[]{:S(2)}, u32[]{:S(2)}) collective-permute-start(f32[32,1,512]{2,1,0:T(1,128)S(1)} %get-tuple-element.150), channel_id=1, source_target_pairs={{0,2},{2,4},{4,6},{6,8},{8,10},{10,12},{12,14},{14,16},{16,18},{18... | collective-permute-start | bytes 196616 | tf_op jit(solution)/shard_map/while/body/ppermute | solution.py:14
  412.6 6.2 %collective-permute-start.1 = (f32[32,1,512]{2,1,0:T(1,128)S(1)}, f32[32,1,512]{2,1,0:T(1,128)S(1)}, u32[]{:S(2)}, u32[]{:S(2)}) collective-permute-start(f32[32,1,512]{2,1,0:T(1,128)S(1)} %get-tuple-element.150), channel_id=1, source_target_pairs={{0,2},{2,4},{4,6},{6,8},{8,10},{10,12},{12,14},{14,16},{16,18},{18... | collective-permute-start | bytes 196616 | tf_op jit(solution)/shard_map/while/body/ppermute | solution.py:14
  426.7 6.2 %collective-permute-start.1 = (f32[32,1,512]{2,1,0:T(1,128)S(1)}, f32[32,1,512]{2,1,0:T(1,128)S(1)}, u32[]{:S(2)}, u32[]{:S(2)}) collective-permute-start(f32[32,1,512]{2,1,0:T(1,128)S(1)} %get-tuple-element.150), channel_id=1, source_target_pairs={{0,2},{2,4},{4,6},{6,8},{8,10},{10,12},{12,14},{14,16},{16,18},{18... | collective-permute-start | bytes 196616 | tf_op jit(solution)/shard_map/while/body/ppermute | solution.py:14
  440.9 6.2 %collective-permute-start.1 = (f32[32,1,512]{2,1,0:T(1,128)S(1)}, f32[32,1,512]{2,1,0:T(1,128)S(1)}, u32[]{:S(2)}, u32[]{:S(2)}) collective-permute-start(f32[32,1,512]{2,1,0:T(1,128)S(1)} %get-tuple-element.150), channel_id=1, source_target_pairs={{0,2},{2,4},{4,6},{6,8},{8,10},{10,12},{12,14},{14,16},{16,18},{18... | collective-permute-start | bytes 196616 | tf_op jit(solution)/shard_map/while/body/ppermute | solution.py:14
  455.0 6.2 %collective-permute-start.1 = (f32[32,1,512]{2,1,0:T(1,128)S(1)}, f32[32,1,512]{2,1,0:T(1,128)S(1)}, u32[]{:S(2)}, u32[]{:S(2)}) collective-permute-start(f32[32,1,512]{2,1,0:T(1,128)S(1)} %get-tuple-element.150), channel_id=1, source_target_pairs={{0,2},{2,4},{4,6},{6,8},{8,10},{10,12},{12,14},{14,16},{16,18},{18... | collective-permute-start | bytes 196616 | tf_op jit(solution)/shard_map/while/body/ppermute | solution.py:14
  481.4 50.6 %all-reduce.2 = (f32[64,64]{1,0:T(8,128)S(1)}, f32[64,64]{1,0:T(8,128)S(1)}) all-reduce(f32[64,64]{1,0:T(8,128)S(1)} %fusion.32, f32[64,64]{1,0:T(8,128)S(1)} %fusion.31), channel_id=1, replica_groups=mesh['space'=16,'ens'=2] {'space','ens'}, use_global_device_ids=true, to_apply=%region_7.8 | all-reduce | flops 8192 | bytes 65536 | tf_op jit(solution)/shard_map/psum | solution.py:83
  532.1 5.8 %cholesky.17 = f32[64,64]{1,0:T(8,128)S(1)} custom-call(f32[64,64]{1,0:T(8,128)S(1)} %fusion.23), custom_call_target="Cholesky" | custom-call | tf_op jit(solution)/shard_map/jit(cholesky)/cholesky | solution.py:51
  (319 shorter events, 290.8 us)
Async XLA Ops:
  7.2 537.7 %all-gather.2.cloned.1.call-start = ((), (), s32[]{:S(2)}) async-start(), calls=%async_computation.1 | async-start | bytes 3145728 | tf_op jit(solution)/shard_map/all_gather | solution.py:86
  47.8 7.4 %collective-permute-start = (f32[32,1,512]{2,1,0:T(1,128)S(1)}, f32[32,1,512]{2,1,0:T(1,128)S(1)}, u32[]{:S(2)}, u32[]{:S(2)}) collective-permute-start(f32[32,1,512]{2,1,0:T(1,128)S(1)} %get-tuple-element.149), channel_id=1, source_target_pairs={{2,0},{4,2},{6,4},{8,6},{10,8},{12,10},{14,12},{16,14},{18,16},{20... | collective-permute-start | bytes 196616 | tf_op jit(solution)/shard_map/while/body/ppermute | solution.py:17
  75.1 7.4 %collective-permute-start = (f32[32,1,512]{2,1,0:T(1,128)S(1)}, f32[32,1,512]{2,1,0:T(1,128)S(1)}, u32[]{:S(2)}, u32[]{:S(2)}) collective-permute-start(f32[32,1,512]{2,1,0:T(1,128)S(1)} %get-tuple-element.149), channel_id=1, source_target_pairs={{2,0},{4,2},{6,4},{8,6},{10,8},{12,10},{14,12},{16,14},{18,16},{20... | collective-permute-start | bytes 196616 | tf_op jit(solution)/shard_map/while/body/ppermute | solution.py:17
  89.0 7.4 %collective-permute-start = (f32[32,1,512]{2,1,0:T(1,128)S(1)}, f32[32,1,512]{2,1,0:T(1,128)S(1)}, u32[]{:S(2)}, u32[]{:S(2)}) collective-permute-start(f32[32,1,512]{2,1,0:T(1,128)S(1)} %get-tuple-element.149), channel_id=1, source_target_pairs={{2,0},{4,2},{6,4},{8,6},{10,8},{12,10},{14,12},{16,14},{18,16},{20... | collective-permute-start | bytes 196616 | tf_op jit(solution)/shard_map/while/body/ppermute | solution.py:17
  142.7 7.5 %collective-permute-start = (f32[32,1,512]{2,1,0:T(1,128)S(1)}, f32[32,1,512]{2,1,0:T(1,128)S(1)}, u32[]{:S(2)}, u32[]{:S(2)}) collective-permute-start(f32[32,1,512]{2,1,0:T(1,128)S(1)} %get-tuple-element.149), channel_id=1, source_target_pairs={{2,0},{4,2},{6,4},{8,6},{10,8},{12,10},{14,12},{16,14},{18,16},{20... | collective-permute-start | bytes 196616 | tf_op jit(solution)/shard_map/while/body/ppermute | solution.py:17
  156.9 7.5 %collective-permute-start = (f32[32,1,512]{2,1,0:T(1,128)S(1)}, f32[32,1,512]{2,1,0:T(1,128)S(1)}, u32[]{:S(2)}, u32[]{:S(2)}) collective-permute-start(f32[32,1,512]{2,1,0:T(1,128)S(1)} %get-tuple-element.149), channel_id=1, source_target_pairs={{2,0},{4,2},{6,4},{8,6},{10,8},{12,10},{14,12},{16,14},{18,16},{20... | collective-permute-start | bytes 196616 | tf_op jit(solution)/shard_map/while/body/ppermute | solution.py:17
  158.2 7.1 %collective-permute-start.1 = (f32[32,1,512]{2,1,0:T(1,128)S(1)}, f32[32,1,512]{2,1,0:T(1,128)S(1)}, u32[]{:S(2)}, u32[]{:S(2)}) collective-permute-start(f32[32,1,512]{2,1,0:T(1,128)S(1)} %get-tuple-element.150), channel_id=1, source_target_pairs={{0,2},{2,4},{4,6},{6,8},{8,10},{10,12},{12,14},{14,16},{16,18},{18... | collective-permute-start | bytes 196616 | tf_op jit(solution)/shard_map/while/body/ppermute | solution.py:14
  171.0 7.5 %collective-permute-start = (f32[32,1,512]{2,1,0:T(1,128)S(1)}, f32[32,1,512]{2,1,0:T(1,128)S(1)}, u32[]{:S(2)}, u32[]{:S(2)}) collective-permute-start(f32[32,1,512]{2,1,0:T(1,128)S(1)} %get-tuple-element.149), channel_id=1, source_target_pairs={{2,0},{4,2},{6,4},{8,6},{10,8},{12,10},{14,12},{16,14},{18,16},{20... | collective-permute-start | bytes 196616 | tf_op jit(solution)/shard_map/while/body/ppermute | solution.py:17
  185.1 7.5 %collective-permute-start = (f32[32,1,512]{2,1,0:T(1,128)S(1)}, f32[32,1,512]{2,1,0:T(1,128)S(1)}, u32[]{:S(2)}, u32[]{:S(2)}) collective-permute-start(f32[32,1,512]{2,1,0:T(1,128)S(1)} %get-tuple-element.149), channel_id=1, source_target_pairs={{2,0},{4,2},{6,4},{8,6},{10,8},{12,10},{14,12},{16,14},{18,16},{20... | collective-permute-start | bytes 196616 | tf_op jit(solution)/shard_map/while/body/ppermute | solution.py:17
  186.4 7.1 %collective-permute-start.1 = (f32[32,1,512]{2,1,0:T(1,128)S(1)}, f32[32,1,512]{2,1,0:T(1,128)S(1)}, u32[]{:S(2)}, u32[]{:S(2)}) collective-permute-start(f32[32,1,512]{2,1,0:T(1,128)S(1)} %get-tuple-element.150), channel_id=1, source_target_pairs={{0,2},{2,4},{4,6},{6,8},{8,10},{10,12},{12,14},{14,16},{16,18},{18... | collective-permute-start | bytes 196616 | tf_op jit(solution)/shard_map/while/body/ppermute | solution.py:14
  199.3 7.5 %collective-permute-start = (f32[32,1,512]{2,1,0:T(1,128)S(1)}, f32[32,1,512]{2,1,0:T(1,128)S(1)}, u32[]{:S(2)}, u32[]{:S(2)}) collective-permute-start(f32[32,1,512]{2,1,0:T(1,128)S(1)} %get-tuple-element.149), channel_id=1, source_target_pairs={{2,0},{4,2},{6,4},{8,6},{10,8},{12,10},{14,12},{16,14},{18,16},{20... | collective-permute-start | bytes 196616 | tf_op jit(solution)/shard_map/while/body/ppermute | solution.py:17
  200.6 7.1 %collective-permute-start.1 = (f32[32,1,512]{2,1,0:T(1,128)S(1)}, f32[32,1,512]{2,1,0:T(1,128)S(1)}, u32[]{:S(2)}, u32[]{:S(2)}) collective-permute-start(f32[32,1,512]{2,1,0:T(1,128)S(1)} %get-tuple-element.150), channel_id=1, source_target_pairs={{0,2},{2,4},{4,6},{6,8},{8,10},{10,12},{12,14},{14,16},{16,18},{18... | collective-permute-start | bytes 196616 | tf_op jit(solution)/shard_map/while/body/ppermute | solution.py:14
  213.4 7.5 %collective-permute-start = (f32[32,1,512]{2,1,0:T(1,128)S(1)}, f32[32,1,512]{2,1,0:T(1,128)S(1)}, u32[]{:S(2)}, u32[]{:S(2)}) collective-permute-start(f32[32,1,512]{2,1,0:T(1,128)S(1)} %get-tuple-element.149), channel_id=1, source_target_pairs={{2,0},{4,2},{6,4},{8,6},{10,8},{12,10},{14,12},{16,14},{18,16},{20... | collective-permute-start | bytes 196616 | tf_op jit(solution)/shard_map/while/body/ppermute | solution.py:17
  214.7 7.1 %collective-permute-start.1 = (f32[32,1,512]{2,1,0:T(1,128)S(1)}, f32[32,1,512]{2,1,0:T(1,128)S(1)}, u32[]{:S(2)}, u32[]{:S(2)}) collective-permute-start(f32[32,1,512]{2,1,0:T(1,128)S(1)} %get-tuple-element.150), channel_id=1, source_target_pairs={{0,2},{2,4},{4,6},{6,8},{8,10},{10,12},{12,14},{14,16},{16,18},{18... | collective-permute-start | bytes 196616 | tf_op jit(solution)/shard_map/while/body/ppermute | solution.py:14
  227.5 7.5 %collective-permute-start = (f32[32,1,512]{2,1,0:T(1,128)S(1)}, f32[32,1,512]{2,1,0:T(1,128)S(1)}, u32[]{:S(2)}, u32[]{:S(2)}) collective-permute-start(f32[32,1,512]{2,1,0:T(1,128)S(1)} %get-tuple-element.149), channel_id=1, source_target_pairs={{2,0},{4,2},{6,4},{8,6},{10,8},{12,10},{14,12},{16,14},{18,16},{20... | collective-permute-start | bytes 196616 | tf_op jit(solution)/shard_map/while/body/ppermute | solution.py:17
  241.7 7.5 %collective-permute-start = (f32[32,1,512]{2,1,0:T(1,128)S(1)}, f32[32,1,512]{2,1,0:T(1,128)S(1)}, u32[]{:S(2)}, u32[]{:S(2)}) collective-permute-start(f32[32,1,512]{2,1,0:T(1,128)S(1)} %get-tuple-element.149), channel_id=1, source_target_pairs={{2,0},{4,2},{6,4},{8,6},{10,8},{12,10},{14,12},{16,14},{18,16},{20... | collective-permute-start | bytes 196616 | tf_op jit(solution)/shard_map/while/body/ppermute | solution.py:17
  255.8 7.5 %collective-permute-start = (f32[32,1,512]{2,1,0:T(1,128)S(1)}, f32[32,1,512]{2,1,0:T(1,128)S(1)}, u32[]{:S(2)}, u32[]{:S(2)}) collective-permute-start(f32[32,1,512]{2,1,0:T(1,128)S(1)} %get-tuple-element.149), channel_id=1, source_target_pairs={{2,0},{4,2},{6,4},{8,6},{10,8},{12,10},{14,12},{16,14},{18,16},{20... | collective-permute-start | bytes 196616 | tf_op jit(solution)/shard_map/while/body/ppermute | solution.py:17
  269.9 7.5 %collective-permute-start = (f32[32,1,512]{2,1,0:T(1,128)S(1)}, f32[32,1,512]{2,1,0:T(1,128)S(1)}, u32[]{:S(2)}, u32[]{:S(2)}) collective-permute-start(f32[32,1,512]{2,1,0:T(1,128)S(1)} %get-tuple-element.149), channel_id=1, source_target_pairs={{2,0},{4,2},{6,4},{8,6},{10,8},{12,10},{14,12},{16,14},{18,16},{20... | collective-permute-start | bytes 196616 | tf_op jit(solution)/shard_map/while/body/ppermute | solution.py:17
  284.1 7.5 %collective-permute-start = (f32[32,1,512]{2,1,0:T(1,128)S(1)}, f32[32,1,512]{2,1,0:T(1,128)S(1)}, u32[]{:S(2)}, u32[]{:S(2)}) collective-permute-start(f32[32,1,512]{2,1,0:T(1,128)S(1)} %get-tuple-element.149), channel_id=1, source_target_pairs={{2,0},{4,2},{6,4},{8,6},{10,8},{12,10},{14,12},{16,14},{18,16},{20... | collective-permute-start | bytes 196616 | tf_op jit(solution)/shard_map/while/body/ppermute | solution.py:17
  298.2 7.5 %collective-permute-start = (f32[32,1,512]{2,1,0:T(1,128)S(1)}, f32[32,1,512]{2,1,0:T(1,128)S(1)}, u32[]{:S(2)}, u32[]{:S(2)}) collective-permute-start(f32[32,1,512]{2,1,0:T(1,128)S(1)} %get-tuple-element.149), channel_id=1, source_target_pairs={{2,0},{4,2},{6,4},{8,6},{10,8},{12,10},{14,12},{16,14},{18,16},{20... | collective-permute-start | bytes 196616 | tf_op jit(solution)/shard_map/while/body/ppermute | solution.py:17
  312.3 7.5 %collective-permute-start = (f32[32,1,512]{2,1,0:T(1,128)S(1)}, f32[32,1,512]{2,1,0:T(1,128)S(1)}, u32[]{:S(2)}, u32[]{:S(2)}) collective-permute-start(f32[32,1,512]{2,1,0:T(1,128)S(1)} %get-tuple-element.149), channel_id=1, source_target_pairs={{2,0},{4,2},{6,4},{8,6},{10,8},{12,10},{14,12},{16,14},{18,16},{20... | collective-permute-start | bytes 196616 | tf_op jit(solution)/shard_map/while/body/ppermute | solution.py:17
  326.5 7.5 %collective-permute-start = (f32[32,1,512]{2,1,0:T(1,128)S(1)}, f32[32,1,512]{2,1,0:T(1,128)S(1)}, u32[]{:S(2)}, u32[]{:S(2)}) collective-permute-start(f32[32,1,512]{2,1,0:T(1,128)S(1)} %get-tuple-element.149), channel_id=1, source_target_pairs={{2,0},{4,2},{6,4},{8,6},{10,8},{12,10},{14,12},{16,14},{18,16},{20... | collective-permute-start | bytes 196616 | tf_op jit(solution)/shard_map/while/body/ppermute | solution.py:17
  340.6 7.5 %collective-permute-start = (f32[32,1,512]{2,1,0:T(1,128)S(1)}, f32[32,1,512]{2,1,0:T(1,128)S(1)}, u32[]{:S(2)}, u32[]{:S(2)}) collective-permute-start(f32[32,1,512]{2,1,0:T(1,128)S(1)} %get-tuple-element.149), channel_id=1, source_target_pairs={{2,0},{4,2},{6,4},{8,6},{10,8},{12,10},{14,12},{16,14},{18,16},{20... | collective-permute-start | bytes 196616 | tf_op jit(solution)/shard_map/while/body/ppermute | solution.py:17
  354.8 7.5 %collective-permute-start = (f32[32,1,512]{2,1,0:T(1,128)S(1)}, f32[32,1,512]{2,1,0:T(1,128)S(1)}, u32[]{:S(2)}, u32[]{:S(2)}) collective-permute-start(f32[32,1,512]{2,1,0:T(1,128)S(1)} %get-tuple-element.149), channel_id=1, source_target_pairs={{2,0},{4,2},{6,4},{8,6},{10,8},{12,10},{14,12},{16,14},{18,16},{20... | collective-permute-start | bytes 196616 | tf_op jit(solution)/shard_map/while/body/ppermute | solution.py:17
  368.9 7.5 %collective-permute-start = (f32[32,1,512]{2,1,0:T(1,128)S(1)}, f32[32,1,512]{2,1,0:T(1,128)S(1)}, u32[]{:S(2)}, u32[]{:S(2)}) collective-permute-start(f32[32,1,512]{2,1,0:T(1,128)S(1)} %get-tuple-element.149), channel_id=1, source_target_pairs={{2,0},{4,2},{6,4},{8,6},{10,8},{12,10},{14,12},{16,14},{18,16},{20... | collective-permute-start | bytes 196616 | tf_op jit(solution)/shard_map/while/body/ppermute | solution.py:17
  383.0 7.5 %collective-permute-start = (f32[32,1,512]{2,1,0:T(1,128)S(1)}, f32[32,1,512]{2,1,0:T(1,128)S(1)}, u32[]{:S(2)}, u32[]{:S(2)}) collective-permute-start(f32[32,1,512]{2,1,0:T(1,128)S(1)} %get-tuple-element.149), channel_id=1, source_target_pairs={{2,0},{4,2},{6,4},{8,6},{10,8},{12,10},{14,12},{16,14},{18,16},{20... | collective-permute-start | bytes 196616 | tf_op jit(solution)/shard_map/while/body/ppermute | solution.py:17
  397.2 7.5 %collective-permute-start = (f32[32,1,512]{2,1,0:T(1,128)S(1)}, f32[32,1,512]{2,1,0:T(1,128)S(1)}, u32[]{:S(2)}, u32[]{:S(2)}) collective-permute-start(f32[32,1,512]{2,1,0:T(1,128)S(1)} %get-tuple-element.149), channel_id=1, source_target_pairs={{2,0},{4,2},{6,4},{8,6},{10,8},{12,10},{14,12},{16,14},{18,16},{20... | collective-permute-start | bytes 196616 | tf_op jit(solution)/shard_map/while/body/ppermute | solution.py:17
  411.3 7.5 %collective-permute-start = (f32[32,1,512]{2,1,0:T(1,128)S(1)}, f32[32,1,512]{2,1,0:T(1,128)S(1)}, u32[]{:S(2)}, u32[]{:S(2)}) collective-permute-start(f32[32,1,512]{2,1,0:T(1,128)S(1)} %get-tuple-element.149), channel_id=1, source_target_pairs={{2,0},{4,2},{6,4},{8,6},{10,8},{12,10},{14,12},{16,14},{18,16},{20... | collective-permute-start | bytes 196616 | tf_op jit(solution)/shard_map/while/body/ppermute | solution.py:17
  425.4 7.5 %collective-permute-start = (f32[32,1,512]{2,1,0:T(1,128)S(1)}, f32[32,1,512]{2,1,0:T(1,128)S(1)}, u32[]{:S(2)}, u32[]{:S(2)}) collective-permute-start(f32[32,1,512]{2,1,0:T(1,128)S(1)} %get-tuple-element.149), channel_id=1, source_target_pairs={{2,0},{4,2},{6,4},{8,6},{10,8},{12,10},{14,12},{16,14},{18,16},{20... | collective-permute-start | bytes 196616 | tf_op jit(solution)/shard_map/while/body/ppermute | solution.py:17
  439.6 7.5 %collective-permute-start = (f32[32,1,512]{2,1,0:T(1,128)S(1)}, f32[32,1,512]{2,1,0:T(1,128)S(1)}, u32[]{:S(2)}, u32[]{:S(2)}) collective-permute-start(f32[32,1,512]{2,1,0:T(1,128)S(1)} %get-tuple-element.149), channel_id=1, source_target_pairs={{2,0},{4,2},{6,4},{8,6},{10,8},{12,10},{14,12},{16,14},{18,16},{20... | collective-permute-start | bytes 196616 | tf_op jit(solution)/shard_map/while/body/ppermute | solution.py:17
  453.7 7.5 %collective-permute-start = (f32[32,1,512]{2,1,0:T(1,128)S(1)}, f32[32,1,512]{2,1,0:T(1,128)S(1)}, u32[]{:S(2)}, u32[]{:S(2)}) collective-permute-start(f32[32,1,512]{2,1,0:T(1,128)S(1)} %get-tuple-element.149), channel_id=1, source_target_pairs={{2,0},{4,2},{6,4},{8,6},{10,8},{12,10},{14,12},{16,14},{18,16},{20... | collective-permute-start | bytes 196616 | tf_op jit(solution)/shard_map/while/body/ppermute | solution.py:17
  473.7 7.2 %all-to-all-start = ((f32[32,2,128]{2,0,1:T(8,128)}), f32[32,2,128]{2,0,1:T(8,128)S(1)}, u32[]{:S(2)}, u32[]{:S(2)}) async-start(f32[32,2,128]{2,0,1:T(8,128)} %broadcast_select_fusion), calls=%async_computation | async-start | bytes 65536 | tf_op jit(solution)/shard_map/all_to_all | solution.py:78
  (44 other events, 298.3 us)
Sparse Core Ops, SparseCore 0:
  9.5 35.8 all-gather.1
where the time goes:
time: 566 us; the launch traced here: 561 us
  starting transfers between devices  242 us (43%)
  other arithmetic  136 us (24%)
  local copies, waits for them, and re-layouts  57.3 us (10%)
  blocking collectives  50.6 us (9%)
  waiting for transfers between devices  35.1 us (6%)
  loops' own time  21.8 us (4%)
  between operations  14.3 us (3%)
    ppermute x33, starting transfers between devices, padded_2(): lax.ppermute(lax.slice_in_dim(block, block.shape[dim] - width, None, axis...  196 us
    select_n x32, other arithmetic, advance(): return jnp.where((step_index < own_counts)[:, None, None], moved, thickness)  87.3 us
    psum x1, blocking collectives, shards(): gram, cross = lax.psum((gram, cross), ('space', 'ens'))  50.6 us
    ppermute x33, starting transfers between devices, padded_2(): lax.ppermute(lax.slice_in_dim(block, 0, width, axis=dim), axis, backward)  42.6 us
    while x32, local copies, waits for them, and re-layouts  39.3 us
    div x32, other arithmetic, stencil(): diffusivity = slip_padded * padded * padded / (1.0 + padded * padded)  32.8 us
    ppermute x33, waiting for transfers between devices, padded_2(): lax.ppermute(lax.slice_in_dim(block, block.shape[dim] - width, None, axis...  27.4 us
    another operation x1, loops' own time, shards(): thickness = lax.fori_loop(0, longest, advance, initial)  21.8 us
  transfers between devices with their start and end apart: 68, of which 34 were waited for; matrix products, arithmetic and copies ran while one was open for 34% of the time, Pallas kernels for 0%

commit v1 on v0

--- a/solution.py
+++ b/solution.py
@@ -1,9 +1,20 @@
+import functools
 import jax
 import jax.numpy as jnp
 from jax import lax
 from jax.sharding import PartitionSpec as P
+from jax.lax import psum
 
 time_step = 0.11
+
+
+def put_space(tile_in, mesh_dim, bus_axis):
+    for rr in (mesh_dim, bus_axis):
+        tile_in = psum(tile_in, axis_name=rr)
+    return tile_in
+
+
+_return_all_turns = functools.partial(put_space, mesh_dim="ens", bus_axis="space")
 
 
 def padded_2(block, sides, width):
@@ -80,7 +91,7 @@
     observed_part = lax.dynamic_slice_in_dim(observed, ens_index * block_width, block_width)
     noise_part = lax.dynamic_slice_in_dim(noise_var, ens_index * block_width, block_width)
     gram, cross = ensemble_terms(obs_block, observed_part, noise_part)
-    gram, cross = lax.psum((gram, cross), ("space", "ens"))
+    gram, cross = _return_all_turns((gram, cross))
     weights = solve_weights(gram, cross)
     weight_cols = lax.dynamic_slice_in_dim(weights, ens_index * members_dev, members_dev, 1)
     piece = lax.all_gather(params, "ens", axis=0, tiled=True)

time: 566 us -> 589 us (1.041)
  blocking collectives: 50.6 us -> 73.8 us
    psum x1 -> x2, blocking collectives: 50.6 us -> 73.8 us  [put_space(): tile_in = psum(tile_in, axis_name=rr)]
  transfers between devices with their start and end apart: 68 -> 68, of which waited for: 34 -> 34; matrix products, arithmetic and copies ran while one was open for 34% -> 32% of each run, Pallas kernels for 0% -> 0%
where the time goes in v1:
time: 589 us; the launch traced here: 585 us
  starting transfers between devices  242 us (41%)
  other arithmetic  136 us (23%)
  blocking collectives  73.8 us (13%)
  local copies, waits for them, and re-layouts  57.3 us (10%)
  waiting for transfers between devices  35.1 us (6%)
  loops' own time  22.7 us (4%)
  between operations  14.3 us (2%)
    ppermute x33, starting transfers between devices, padded_2(): lax.ppermute(lax.slice_in_dim(block, block.shape[dim] - width, None, axis...  196 us
    select_n x32, other arithmetic, advance(): return jnp.where((step_index < own_counts)[:, None, None], moved, thickness)  87.3 us
    psum x2, blocking collectives, put_space(): tile_in = psum(tile_in, axis_name=rr)  73.8 us
    ppermute x33, starting transfers between devices, padded_2(): lax.ppermute(lax.slice_in_dim(block, 0, width, axis=dim), axis, backward)  42.6 us
    while x32, local copies, waits for them, and re-layouts  39.3 us
    div x32, other arithmetic, stencil(): diffusivity = slip_padded * padded * padded / (1.0 + padded * padded)  32.8 us
    ppermute x33, waiting for transfers between devices, padded_2(): lax.ppermute(lax.slice_in_dim(block, block.shape[dim] - width, None, axis...  27.4 us
    another operation x1, loops' own time, shards(): thickness = lax.fori_loop(0, longest, advance, initial)  22.7 us
  transfers between devices with their start and end apart: 68, of which 34 were waited for; matrix products, arithmetic and copies ran while one was open for 32% of the time, Pallas kernels for 0%

profile of v1, /device:TPU:0, one launch (start us, length us, event | category | flops | bytes accessed | tf_op | source)
XLA Modules:
  0.0 584.9 jit_solution(14355301836889301861)
XLA Ops:
  19.3 448.1 %while.12 = (s32[]{:T(128)}, f32[32,16,512]{2,1,0:T(8,128)}, s32[]{:T(128)}, s32[32]{0:T(128)S(1)}, f32[32,18,514]{2,1,0:T(8,128)S(1)}, /*index=5*/f32[16,512]{1,0:T(8,128)S(1)}, s32[]{:T(128)}) while((s32[]{:T(128)}, f32[32,16,512]{2,1,0:T(8,128)}, s32[]{:T(128)}, s32[32]{0:T(128)S(1)}, f32[32,18,514]{2,1,0:T(8,128)S(1)}, ...), condition=%wide.region_2.3_spmd, body=%wide.region_1.2_spmd.sunk | while | flops 10402466 | bytes 17217376 | solution.py:86
  22.6 5.4 collective-permute-start.1
  49.2 6.0 %collective-permute-start.1 = (f32[32,1,512]{2,1,0:T(1,128)S(1)}, f32[32,1,512]{2,1,0:T(1,128)S(1)}, u32[]{:S(2)}, u32[]{:S(2)}) collective-permute-start(f32[32,1,512]{2,1,0:T(1,128)S(1)} %get-tuple-element.152), channel_id=1, source_target_pairs={{0,2},{2,4},{4,6},{6,8},{8,10},{10,12},{12,14},{14,16},{16,18},{18... | collective-permute-start | bytes 196616 | tf_op jit(solution)/shard_map/while/body/ppermute | solution.py:25
  63.2 5.4 collective-permute-start.1
  76.5 6.0 %collective-permute-start.1 = (f32[32,1,512]{2,1,0:T(1,128)S(1)}, f32[32,1,512]{2,1,0:T(1,128)S(1)}, u32[]{:S(2)}, u32[]{:S(2)}) collective-permute-start(f32[32,1,512]{2,1,0:T(1,128)S(1)} %get-tuple-element.152), channel_id=1, source_target_pairs={{0,2},{2,4},{4,6},{6,8},{8,10},{10,12},{12,14},{14,16},{16,18},{18... | collective-permute-start | bytes 196616 | tf_op jit(solution)/shard_map/while/body/ppermute | solution.py:25
  90.5 6.0 %collective-permute-start.1 = (f32[32,1,512]{2,1,0:T(1,128)S(1)}, f32[32,1,512]{2,1,0:T(1,128)S(1)}, u32[]{:S(2)}, u32[]{:S(2)}) collective-permute-start(f32[32,1,512]{2,1,0:T(1,128)S(1)} %get-tuple-element.152), channel_id=1, source_target_pairs={{0,2},{2,4},{4,6},{6,8},{8,10},{10,12},{12,14},{14,16},{16,18},{18... | collective-permute-start | bytes 196616 | tf_op jit(solution)/shard_map/while/body/ppermute | solution.py:25
  144.3 6.2 %collective-permute-start.1 = (f32[32,1,512]{2,1,0:T(1,128)S(1)}, f32[32,1,512]{2,1,0:T(1,128)S(1)}, u32[]{:S(2)}, u32[]{:S(2)}) collective-permute-start(f32[32,1,512]{2,1,0:T(1,128)S(1)} %get-tuple-element.152), channel_id=1, source_target_pairs={{0,2},{2,4},{4,6},{6,8},{8,10},{10,12},{12,14},{14,16},{16,18},{18... | collective-permute-start | bytes 196616 | tf_op jit(solution)/shard_map/while/body/ppermute | solution.py:25
  158.4 6.2 %collective-permute-start.1 = (f32[32,1,512]{2,1,0:T(1,128)S(1)}, f32[32,1,512]{2,1,0:T(1,128)S(1)}, u32[]{:S(2)}, u32[]{:S(2)}) collective-permute-start(f32[32,1,512]{2,1,0:T(1,128)S(1)} %get-tuple-element.152), channel_id=1, source_target_pairs={{0,2},{2,4},{4,6},{6,8},{8,10},{10,12},{12,14},{14,16},{16,18},{18... | collective-permute-start | bytes 196616 | tf_op jit(solution)/shard_map/while/body/ppermute | solution.py:25
  172.6 6.2 %collective-permute-start.1 = (f32[32,1,512]{2,1,0:T(1,128)S(1)}, f32[32,1,512]{2,1,0:T(1,128)S(1)}, u32[]{:S(2)}, u32[]{:S(2)}) collective-permute-start(f32[32,1,512]{2,1,0:T(1,128)S(1)} %get-tuple-element.152), channel_id=1, source_target_pairs={{0,2},{2,4},{4,6},{6,8},{8,10},{10,12},{12,14},{14,16},{16,18},{18... | collective-permute-start | bytes 196616 | tf_op jit(solution)/shard_map/while/body/ppermute | solution.py:25
  186.8 6.2 %collective-permute-start.1 = (f32[32,1,512]{2,1,0:T(1,128)S(1)}, f32[32,1,512]{2,1,0:T(1,128)S(1)}, u32[]{:S(2)}, u32[]{:S(2)}) collective-permute-start(f32[32,1,512]{2,1,0:T(1,128)S(1)} %get-tuple-element.152), channel_id=1, source_target_pairs={{0,2},{2,4},{4,6},{6,8},{8,10},{10,12},{12,14},{14,16},{16,18},{18... | collective-permute-start | bytes 196616 | tf_op jit(solution)/shard_map/while/body/ppermute | solution.py:25
  200.9 6.2 %collective-permute-start.1 = (f32[32,1,512]{2,1,0:T(1,128)S(1)}, f32[32,1,512]{2,1,0:T(1,128)S(1)}, u32[]{:S(2)}, u32[]{:S(2)}) collective-permute-start(f32[32,1,512]{2,1,0:T(1,128)S(1)} %get-tuple-element.152), channel_id=1, source_target_pairs={{0,2},{2,4},{4,6},{6,8},{8,10},{10,12},{12,14},{14,16},{16,18},{18... | collective-permute-start | bytes 196616 | tf_op jit(solution)/shard_map/while/body/ppermute | solution.py:25
  215.1 6.2 %collective-permute-start.1 = (f32[32,1,512]{2,1,0:T(1,128)S(1)}, f32[32,1,512]{2,1,0:T(1,128)S(1)}, u32[]{:S(2)}, u32[]{:S(2)}) collective-permute-start(f32[32,1,512]{2,1,0:T(1,128)S(1)} %get-tuple-element.152), channel_id=1, source_target_pairs={{0,2},{2,4},{4,6},{6,8},{8,10},{10,12},{12,14},{14,16},{16,18},{18... | collective-permute-start | bytes 196616 | tf_op jit(solution)/shard_map/while/body/ppermute | solution.py:25
  229.3 6.2 %collective-permute-start.1 = (f32[32,1,512]{2,1,0:T(1,128)S(1)}, f32[32,1,512]{2,1,0:T(1,128)S(1)}, u32[]{:S(2)}, u32[]{:S(2)}) collective-permute-start(f32[32,1,512]{2,1,0:T(1,128)S(1)} %get-tuple-element.152), channel_id=1, source_target_pairs={{0,2},{2,4},{4,6},{6,8},{8,10},{10,12},{12,14},{14,16},{16,18},{18... | collective-permute-start | bytes 196616 | tf_op jit(solution)/shard_map/while/body/ppermute | solution.py:25
  243.4 6.2 %collective-permute-start.1 = (f32[32,1,512]{2,1,0:T(1,128)S(1)}, f32[32,1,512]{2,1,0:T(1,128)S(1)}, u32[]{:S(2)}, u32[]{:S(2)}) collective-permute-start(f32[32,1,512]{2,1,0:T(1,128)S(1)} %get-tuple-element.152), channel_id=1, source_target_pairs={{0,2},{2,4},{4,6},{6,8},{8,10},{10,12},{12,14},{14,16},{16,18},{18... | collective-permute-start | bytes 196616 | tf_op jit(solution)/shard_map/while/body/ppermute | solution.py:25
  257.6 6.2 %collective-permute-start.1 = (f32[32,1,512]{2,1,0:T(1,128)S(1)}, f32[32,1,512]{2,1,0:T(1,128)S(1)}, u32[]{:S(2)}, u32[]{:S(2)}) collective-permute-start(f32[32,1,512]{2,1,0:T(1,128)S(1)} %get-tuple-element.152), channel_id=1, source_target_pairs={{0,2},{2,4},{4,6},{6,8},{8,10},{10,12},{12,14},{14,16},{16,18},{18... | collective-permute-start | bytes 196616 | tf_op jit(solution)/shard_map/while/body/ppermute | solution.py:25
  271.7 6.2 %collective-permute-start.1 = (f32[32,1,512]{2,1,0:T(1,128)S(1)}, f32[32,1,512]{2,1,0:T(1,128)S(1)}, u32[]{:S(2)}, u32[]{:S(2)}) collective-permute-start(f32[32,1,512]{2,1,0:T(1,128)S(1)} %get-tuple-element.152), channel_id=1, source_target_pairs={{0,2},{2,4},{4,6},{6,8},{8,10},{10,12},{12,14},{14,16},{16,18},{18... | collective-permute-start | bytes 196616 | tf_op jit(solution)/shard_map/while/body/ppermute | solution.py:25
  285.9 6.2 %collective-permute-start.1 = (f32[32,1,512]{2,1,0:T(1,128)S(1)}, f32[32,1,512]{2,1,0:T(1,128)S(1)}, u32[]{:S(2)}, u32[]{:S(2)}) collective-permute-start(f32[32,1,512]{2,1,0:T(1,128)S(1)} %get-tuple-element.152), channel_id=1, source_target_pairs={{0,2},{2,4},{4,6},{6,8},{8,10},{10,12},{12,14},{14,16},{16,18},{18... | collective-permute-start | bytes 196616 | tf_op jit(solution)/shard_map/while/body/ppermute | solution.py:25
  300.1 6.2 %collective-permute-start.1 = (f32[32,1,512]{2,1,0:T(1,128)S(1)}, f32[32,1,512]{2,1,0:T(1,128)S(1)}, u32[]{:S(2)}, u32[]{:S(2)}) collective-permute-start(f32[32,1,512]{2,1,0:T(1,128)S(1)} %get-tuple-element.152), channel_id=1, source_target_pairs={{0,2},{2,4},{4,6},{6,8},{8,10},{10,12},{12,14},{14,16},{16,18},{18... | collective-permute-start | bytes 196616 | tf_op jit(solution)/shard_map/while/body/ppermute | solution.py:25
  314.2 6.2 %collective-permute-start.1 = (f32[32,1,512]{2,1,0:T(1,128)S(1)}, f32[32,1,512]{2,1,0:T(1,128)S(1)}, u32[]{:S(2)}, u32[]{:S(2)}) collective-permute-start(f32[32,1,512]{2,1,0:T(1,128)S(1)} %get-tuple-element.152), channel_id=1, source_target_pairs={{0,2},{2,4},{4,6},{6,8},{8,10},{10,12},{12,14},{14,16},{16,18},{18... | collective-permute-start | bytes 196616 | tf_op jit(solution)/shard_map/while/body/ppermute | solution.py:25
  328.4 6.2 %collective-permute-start.1 = (f32[32,1,512]{2,1,0:T(1,128)S(1)}, f32[32,1,512]{2,1,0:T(1,128)S(1)}, u32[]{:S(2)}, u32[]{:S(2)}) collective-permute-start(f32[32,1,512]{2,1,0:T(1,128)S(1)} %get-tuple-element.152), channel_id=1, source_target_pairs={{0,2},{2,4},{4,6},{6,8},{8,10},{10,12},{12,14},{14,16},{16,18},{18... | collective-permute-start | bytes 196616 | tf_op jit(solution)/shard_map/while/body/ppermute | solution.py:25
  342.6 6.2 %collective-permute-start.1 = (f32[32,1,512]{2,1,0:T(1,128)S(1)}, f32[32,1,512]{2,1,0:T(1,128)S(1)}, u32[]{:S(2)}, u32[]{:S(2)}) collective-permute-start(f32[32,1,512]{2,1,0:T(1,128)S(1)} %get-tuple-element.152), channel_id=1, source_target_pairs={{0,2},{2,4},{4,6},{6,8},{8,10},{10,12},{12,14},{14,16},{16,18},{18... | collective-permute-start | bytes 196616 | tf_op jit(solution)/shard_map/while/body/ppermute | solution.py:25
  356.7 6.2 %collective-permute-start.1 = (f32[32,1,512]{2,1,0:T(1,128)S(1)}, f32[32,1,512]{2,1,0:T(1,128)S(1)}, u32[]{:S(2)}, u32[]{:S(2)}) collective-permute-start(f32[32,1,512]{2,1,0:T(1,128)S(1)} %get-tuple-element.152), channel_id=1, source_target_pairs={{0,2},{2,4},{4,6},{6,8},{8,10},{10,12},{12,14},{14,16},{16,18},{18... | collective-permute-start | bytes 196616 | tf_op jit(solution)/shard_map/while/body/ppermute | solution.py:25
  370.9 6.2 %collective-permute-start.1 = (f32[32,1,512]{2,1,0:T(1,128)S(1)}, f32[32,1,512]{2,1,0:T(1,128)S(1)}, u32[]{:S(2)}, u32[]{:S(2)}) collective-permute-start(f32[32,1,512]{2,1,0:T(1,128)S(1)} %get-tuple-element.152), channel_id=1, source_target_pairs={{0,2},{2,4},{4,6},{6,8},{8,10},{10,12},{12,14},{14,16},{16,18},{18... | collective-permute-start | bytes 196616 | tf_op jit(solution)/shard_map/while/body/ppermute | solution.py:25
  385.1 6.2 %collective-permute-start.1 = (f32[32,1,512]{2,1,0:T(1,128)S(1)}, f32[32,1,512]{2,1,0:T(1,128)S(1)}, u32[]{:S(2)}, u32[]{:S(2)}) collective-permute-start(f32[32,1,512]{2,1,0:T(1,128)S(1)} %get-tuple-element.152), channel_id=1, source_target_pairs={{0,2},{2,4},{4,6},{6,8},{8,10},{10,12},{12,14},{14,16},{16,18},{18... | collective-permute-start | bytes 196616 | tf_op jit(solution)/shard_map/while/body/ppermute | solution.py:25
  399.2 6.2 %collective-permute-start.1 = (f32[32,1,512]{2,1,0:T(1,128)S(1)}, f32[32,1,512]{2,1,0:T(1,128)S(1)}, u32[]{:S(2)}, u32[]{:S(2)}) collective-permute-start(f32[32,1,512]{2,1,0:T(1,128)S(1)} %get-tuple-element.152), channel_id=1, source_target_pairs={{0,2},{2,4},{4,6},{6,8},{8,10},{10,12},{12,14},{14,16},{16,18},{18... | collective-permute-start | bytes 196616 | tf_op jit(solution)/shard_map/while/body/ppermute | solution.py:25
  413.4 6.2 %collective-permute-start.1 = (f32[32,1,512]{2,1,0:T(1,128)S(1)}, f32[32,1,512]{2,1,0:T(1,128)S(1)}, u32[]{:S(2)}, u32[]{:S(2)}) collective-permute-start(f32[32,1,512]{2,1,0:T(1,128)S(1)} %get-tuple-element.152), channel_id=1, source_target_pairs={{0,2},{2,4},{4,6},{6,8},{8,10},{10,12},{12,14},{14,16},{16,18},{18... | collective-permute-start | bytes 196616 | tf_op jit(solution)/shard_map/while/body/ppermute | solution.py:25
  427.5 6.2 %collective-permute-start.1 = (f32[32,1,512]{2,1,0:T(1,128)S(1)}, f32[32,1,512]{2,1,0:T(1,128)S(1)}, u32[]{:S(2)}, u32[]{:S(2)}) collective-permute-start(f32[32,1,512]{2,1,0:T(1,128)S(1)} %get-tuple-element.152), channel_id=1, source_target_pairs={{0,2},{2,4},{4,6},{6,8},{8,10},{10,12},{12,14},{14,16},{16,18},{18... | collective-permute-start | bytes 196616 | tf_op jit(solution)/shard_map/while/body/ppermute | solution.py:25
  441.7 6.2 %collective-permute-start.1 = (f32[32,1,512]{2,1,0:T(1,128)S(1)}, f32[32,1,512]{2,1,0:T(1,128)S(1)}, u32[]{:S(2)}, u32[]{:S(2)}) collective-permute-start(f32[32,1,512]{2,1,0:T(1,128)S(1)} %get-tuple-element.152), channel_id=1, source_target_pairs={{0,2},{2,4},{4,6},{6,8},{8,10},{10,12},{12,14},{14,16},{16,18},{18... | collective-permute-start | bytes 196616 | tf_op jit(solution)/shard_map/while/body/ppermute | solution.py:25
  455.9 6.2 %collective-permute-start.1 = (f32[32,1,512]{2,1,0:T(1,128)S(1)}, f32[32,1,512]{2,1,0:T(1,128)S(1)}, u32[]{:S(2)}, u32[]{:S(2)}) collective-permute-start(f32[32,1,512]{2,1,0:T(1,128)S(1)} %get-tuple-element.152), channel_id=1, source_target_pairs={{0,2},{2,4},{4,6},{6,8},{8,10},{10,12},{12,14},{14,16},{16,18},{18... | collective-permute-start | bytes 196616 | tf_op jit(solution)/shard_map/while/body/ppermute | solution.py:25
  482.2 7.4 %all-reduce.3 = (f32[64,64]{1,0:T(8,128)S(1)}, f32[64,64]{1,0:T(8,128)S(1)}) all-reduce(f32[64,64]{1,0:T(8,128)S(1)} %fusion.32, f32[64,64]{1,0:T(8,128)S(1)} %fusion.31), channel_id=1, replica_groups=mesh['space'=16,'ens'=2] {'ens'}, use_global_device_ids=true, to_apply=%region_8.9 | all-reduce | flops 8192 | bytes 65536 | tf_op jit(solution)/shard_map/psum | solution.py:13
  489.6 66.5 %all-reduce.2 = (f32[64,64]{1,0:T(8,128)S(1)}, f32[64,64]{1,0:T(8,128)S(1)}) all-reduce(f32[64,64]{1,0:T(8,128)S(1)} %get-tuple-element.97, f32[64,64]{1,0:T(8,128)S(1)} %get-tuple-element.98), channel_id=1, replica_groups=mesh['space'=16,'ens'=2] {'space'}, use_global_device_ids=true, to_apply=%region_9.10 | all-reduce | flops 8192 | bytes 65536 | tf_op jit(solution)/shard_map/psum | solution.py:13
  556.2 5.8 cholesky.17
  (320 shorter events, 296.2 us)
Async XLA Ops:
  7.2 561.7 %all-gather.2.cloned.1.call-start = ((), (), s32[]{:S(2)}) async-start(), calls=%async_computation.1 | async-start | bytes 3145728 | tf_op jit(solution)/shard_map/all_gather | solution.py:97
  47.9 7.4 %collective-permute-start = (f32[32,1,512]{2,1,0:T(1,128)S(1)}, f32[32,1,512]{2,1,0:T(1,128)S(1)}, u32[]{:S(2)}, u32[]{:S(2)}) collective-permute-start(f32[32,1,512]{2,1,0:T(1,128)S(1)} %get-tuple-element.151), channel_id=1, source_target_pairs={{2,0},{4,2},{6,4},{8,6},{10,8},{12,10},{14,12},{16,14},{18,16},{20... | collective-permute-start | bytes 196616 | tf_op jit(solution)/shard_map/while/body/ppermute | solution.py:28
  75.2 7.4 %collective-permute-start = (f32[32,1,512]{2,1,0:T(1,128)S(1)}, f32[32,1,512]{2,1,0:T(1,128)S(1)}, u32[]{:S(2)}, u32[]{:S(2)}) collective-permute-start(f32[32,1,512]{2,1,0:T(1,128)S(1)} %get-tuple-element.151), channel_id=1, source_target_pairs={{2,0},{4,2},{6,4},{8,6},{10,8},{12,10},{14,12},{16,14},{18,16},{20... | collective-permute-start | bytes 196616 | tf_op jit(solution)/shard_map/while/body/ppermute | solution.py:28
  89.2 7.4 %collective-permute-start = (f32[32,1,512]{2,1,0:T(1,128)S(1)}, f32[32,1,512]{2,1,0:T(1,128)S(1)}, u32[]{:S(2)}, u32[]{:S(2)}) collective-permute-start(f32[32,1,512]{2,1,0:T(1,128)S(1)} %get-tuple-element.151), channel_id=1, source_target_pairs={{2,0},{4,2},{6,4},{8,6},{10,8},{12,10},{14,12},{16,14},{18,16},{20... | collective-permute-start | bytes 196616 | tf_op jit(solution)/shard_map/while/body/ppermute | solution.py:28
  143.0 7.5 %collective-permute-start = (f32[32,1,512]{2,1,0:T(1,128)S(1)}, f32[32,1,512]{2,1,0:T(1,128)S(1)}, u32[]{:S(2)}, u32[]{:S(2)}) collective-permute-start(f32[32,1,512]{2,1,0:T(1,128)S(1)} %get-tuple-element.151), channel_id=1, source_target_pairs={{2,0},{4,2},{6,4},{8,6},{10,8},{12,10},{14,12},{16,14},{18,16},{20... | collective-permute-start | bytes 196616 | tf_op jit(solution)/shard_map/while/body/ppermute | solution.py:28
  157.1 7.5 %collective-permute-start = (f32[32,1,512]{2,1,0:T(1,128)S(1)}, f32[32,1,512]{2,1,0:T(1,128)S(1)}, u32[]{:S(2)}, u32[]{:S(2)}) collective-permute-start(f32[32,1,512]{2,1,0:T(1,128)S(1)} %get-tuple-element.151), channel_id=1, source_target_pairs={{2,0},{4,2},{6,4},{8,6},{10,8},{12,10},{14,12},{16,14},{18,16},{20... | collective-permute-start | bytes 196616 | tf_op jit(solution)/shard_map/while/body/ppermute | solution.py:28
  158.4 7.1 %collective-permute-start.1 = (f32[32,1,512]{2,1,0:T(1,128)S(1)}, f32[32,1,512]{2,1,0:T(1,128)S(1)}, u32[]{:S(2)}, u32[]{:S(2)}) collective-permute-start(f32[32,1,512]{2,1,0:T(1,128)S(1)} %get-tuple-element.152), channel_id=1, source_target_pairs={{0,2},{2,4},{4,6},{6,8},{8,10},{10,12},{12,14},{14,16},{16,18},{18... | collective-permute-start | bytes 196616 | tf_op jit(solution)/shard_map/while/body/ppermute | solution.py:25
  171.3 7.5 %collective-permute-start = (f32[32,1,512]{2,1,0:T(1,128)S(1)}, f32[32,1,512]{2,1,0:T(1,128)S(1)}, u32[]{:S(2)}, u32[]{:S(2)}) collective-permute-start(f32[32,1,512]{2,1,0:T(1,128)S(1)} %get-tuple-element.151), channel_id=1, source_target_pairs={{2,0},{4,2},{6,4},{8,6},{10,8},{12,10},{14,12},{16,14},{18,16},{20... | collective-permute-start | bytes 196616 | tf_op jit(solution)/shard_map/while/body/ppermute | solution.py:28
  185.5 7.5 %collective-permute-start = (f32[32,1,512]{2,1,0:T(1,128)S(1)}, f32[32,1,512]{2,1,0:T(1,128)S(1)}, u32[]{:S(2)}, u32[]{:S(2)}) collective-permute-start(f32[32,1,512]{2,1,0:T(1,128)S(1)} %get-tuple-element.151), channel_id=1, source_target_pairs={{2,0},{4,2},{6,4},{8,6},{10,8},{12,10},{14,12},{16,14},{18,16},{20... | collective-permute-start | bytes 196616 | tf_op jit(solution)/shard_map/while/body/ppermute | solution.py:28
  186.8 7.1 %collective-permute-start.1 = (f32[32,1,512]{2,1,0:T(1,128)S(1)}, f32[32,1,512]{2,1,0:T(1,128)S(1)}, u32[]{:S(2)}, u32[]{:S(2)}) collective-permute-start(f32[32,1,512]{2,1,0:T(1,128)S(1)} %get-tuple-element.152), channel_id=1, source_target_pairs={{0,2},{2,4},{4,6},{6,8},{8,10},{10,12},{12,14},{14,16},{16,18},{18... | collective-permute-start | bytes 196616 | tf_op jit(solution)/shard_map/while/body/ppermute | solution.py:25
  199.6 7.5 %collective-permute-start = (f32[32,1,512]{2,1,0:T(1,128)S(1)}, f32[32,1,512]{2,1,0:T(1,128)S(1)}, u32[]{:S(2)}, u32[]{:S(2)}) collective-permute-start(f32[32,1,512]{2,1,0:T(1,128)S(1)} %get-tuple-element.151), channel_id=1, source_target_pairs={{2,0},{4,2},{6,4},{8,6},{10,8},{12,10},{14,12},{16,14},{18,16},{20... | collective-permute-start | bytes 196616 | tf_op jit(solution)/shard_map/while/body/ppermute | solution.py:28
  200.9 7.1 %collective-permute-start.1 = (f32[32,1,512]{2,1,0:T(1,128)S(1)}, f32[32,1,512]{2,1,0:T(1,128)S(1)}, u32[]{:S(2)}, u32[]{:S(2)}) collective-permute-start(f32[32,1,512]{2,1,0:T(1,128)S(1)} %get-tuple-element.152), channel_id=1, source_target_pairs={{0,2},{2,4},{4,6},{6,8},{8,10},{10,12},{12,14},{14,16},{16,18},{18... | collective-permute-start | bytes 196616 | tf_op jit(solution)/shard_map/while/body/ppermute | solution.py:25
  213.8 7.5 %collective-permute-start = (f32[32,1,512]{2,1,0:T(1,128)S(1)}, f32[32,1,512]{2,1,0:T(1,128)S(1)}, u32[]{:S(2)}, u32[]{:S(2)}) collective-permute-start(f32[32,1,512]{2,1,0:T(1,128)S(1)} %get-tuple-element.151), channel_id=1, source_target_pairs={{2,0},{4,2},{6,4},{8,6},{10,8},{12,10},{14,12},{16,14},{18,16},{20... | collective-permute-start | bytes 196616 | tf_op jit(solution)/shard_map/while/body/ppermute | solution.py:28
  228.0 7.5 %collective-permute-start = (f32[32,1,512]{2,1,0:T(1,128)S(1)}, f32[32,1,512]{2,1,0:T(1,128)S(1)}, u32[]{:S(2)}, u32[]{:S(2)}) collective-permute-start(f32[32,1,512]{2,1,0:T(1,128)S(1)} %get-tuple-element.151), channel_id=1, source_target_pairs={{2,0},{4,2},{6,4},{8,6},{10,8},{12,10},{14,12},{16,14},{18,16},{20... | collective-permute-start | bytes 196616 | tf_op jit(solution)/shard_map/while/body/ppermute | solution.py:28
  229.3 7.1 %collective-permute-start.1 = (f32[32,1,512]{2,1,0:T(1,128)S(1)}, f32[32,1,512]{2,1,0:T(1,128)S(1)}, u32[]{:S(2)}, u32[]{:S(2)}) collective-permute-start(f32[32,1,512]{2,1,0:T(1,128)S(1)} %get-tuple-element.152), channel_id=1, source_target_pairs={{0,2},{2,4},{4,6},{6,8},{8,10},{10,12},{12,14},{14,16},{16,18},{18... | collective-permute-start | bytes 196616 | tf_op jit(solution)/shard_map/while/body/ppermute | solution.py:25
  242.1 7.5 %collective-permute-start = (f32[32,1,512]{2,1,0:T(1,128)S(1)}, f32[32,1,512]{2,1,0:T(1,128)S(1)}, u32[]{:S(2)}, u32[]{:S(2)}) collective-permute-start(f32[32,1,512]{2,1,0:T(1,128)S(1)} %get-tuple-element.151), channel_id=1, source_target_pairs={{2,0},{4,2},{6,4},{8,6},{10,8},{12,10},{14,12},{16,14},{18,16},{20... | collective-permute-start | bytes 196616 | tf_op jit(solution)/shard_map/while/body/ppermute | solution.py:28
  256.3 7.5 %collective-permute-start = (f32[32,1,512]{2,1,0:T(1,128)S(1)}, f32[32,1,512]{2,1,0:T(1,128)S(1)}, u32[]{:S(2)}, u32[]{:S(2)}) collective-permute-start(f32[32,1,512]{2,1,0:T(1,128)S(1)} %get-tuple-element.151), channel_id=1, source_target_pairs={{2,0},{4,2},{6,4},{8,6},{10,8},{12,10},{14,12},{16,14},{18,16},{20... | collective-permute-start | bytes 196616 | tf_op jit(solution)/shard_map/while/body/ppermute | solution.py:28
  270.4 7.5 %collective-permute-start = (f32[32,1,512]{2,1,0:T(1,128)S(1)}, f32[32,1,512]{2,1,0:T(1,128)S(1)}, u32[]{:S(2)}, u32[]{:S(2)}) collective-permute-start(f32[32,1,512]{2,1,0:T(1,128)S(1)} %get-tuple-element.151), channel_id=1, source_target_pairs={{2,0},{4,2},{6,4},{8,6},{10,8},{12,10},{14,12},{16,14},{18,16},{20... | collective-permute-start | bytes 196616 | tf_op jit(solution)/shard_map/while/body/ppermute | solution.py:28
  284.6 7.5 %collective-permute-start = (f32[32,1,512]{2,1,0:T(1,128)S(1)}, f32[32,1,512]{2,1,0:T(1,128)S(1)}, u32[]{:S(2)}, u32[]{:S(2)}) collective-permute-start(f32[32,1,512]{2,1,0:T(1,128)S(1)} %get-tuple-element.151), channel_id=1, source_target_pairs={{2,0},{4,2},{6,4},{8,6},{10,8},{12,10},{14,12},{16,14},{18,16},{20... | collective-permute-start | bytes 196616 | tf_op jit(solution)/shard_map/while/body/ppermute | solution.py:28
  298.8 7.5 %collective-permute-start = (f32[32,1,512]{2,1,0:T(1,128)S(1)}, f32[32,1,512]{2,1,0:T(1,128)S(1)}, u32[]{:S(2)}, u32[]{:S(2)}) collective-permute-start(f32[32,1,512]{2,1,0:T(1,128)S(1)} %get-tuple-element.151), channel_id=1, source_target_pairs={{2,0},{4,2},{6,4},{8,6},{10,8},{12,10},{14,12},{16,14},{18,16},{20... | collective-permute-start | bytes 196616 | tf_op jit(solution)/shard_map/while/body/ppermute | solution.py:28
  312.9 7.5 %collective-permute-start = (f32[32,1,512]{2,1,0:T(1,128)S(1)}, f32[32,1,512]{2,1,0:T(1,128)S(1)}, u32[]{:S(2)}, u32[]{:S(2)}) collective-permute-start(f32[32,1,512]{2,1,0:T(1,128)S(1)} %get-tuple-element.151), channel_id=1, source_target_pairs={{2,0},{4,2},{6,4},{8,6},{10,8},{12,10},{14,12},{16,14},{18,16},{20... | collective-permute-start | bytes 196616 | tf_op jit(solution)/shard_map/while/body/ppermute | solution.py:28
  327.1 7.5 %collective-permute-start = (f32[32,1,512]{2,1,0:T(1,128)S(1)}, f32[32,1,512]{2,1,0:T(1,128)S(1)}, u32[]{:S(2)}, u32[]{:S(2)}) collective-permute-start(f32[32,1,512]{2,1,0:T(1,128)S(1)} %get-tuple-element.151), channel_id=1, source_target_pairs={{2,0},{4,2},{6,4},{8,6},{10,8},{12,10},{14,12},{16,14},{18,16},{20... | collective-permute-start | bytes 196616 | tf_op jit(solution)/shard_map/while/body/ppermute | solution.py:28
  341.3 7.5 %collective-permute-start = (f32[32,1,512]{2,1,0:T(1,128)S(1)}, f32[32,1,512]{2,1,0:T(1,128)S(1)}, u32[]{:S(2)}, u32[]{:S(2)}) collective-permute-start(f32[32,1,512]{2,1,0:T(1,128)S(1)} %get-tuple-element.151), channel_id=1, source_target_pairs={{2,0},{4,2},{6,4},{8,6},{10,8},{12,10},{14,12},{16,14},{18,16},{20... | collective-permute-start | bytes 196616 | tf_op jit(solution)/shard_map/while/body/ppermute | solution.py:28
  355.4 7.5 %collective-permute-start = (f32[32,1,512]{2,1,0:T(1,128)S(1)}, f32[32,1,512]{2,1,0:T(1,128)S(1)}, u32[]{:S(2)}, u32[]{:S(2)}) collective-permute-start(f32[32,1,512]{2,1,0:T(1,128)S(1)} %get-tuple-element.151), channel_id=1, source_target_pairs={{2,0},{4,2},{6,4},{8,6},{10,8},{12,10},{14,12},{16,14},{18,16},{20... | collective-permute-start | bytes 196616 | tf_op jit(solution)/shard_map/while/body/ppermute | solution.py:28
  369.6 7.5 %collective-permute-start = (f32[32,1,512]{2,1,0:T(1,128)S(1)}, f32[32,1,512]{2,1,0:T(1,128)S(1)}, u32[]{:S(2)}, u32[]{:S(2)}) collective-permute-start(f32[32,1,512]{2,1,0:T(1,128)S(1)} %get-tuple-element.151), channel_id=1, source_target_pairs={{2,0},{4,2},{6,4},{8,6},{10,8},{12,10},{14,12},{16,14},{18,16},{20... | collective-permute-start | bytes 196616 | tf_op jit(solution)/shard_map/while/body/ppermute | solution.py:28
  383.8 7.5 %collective-permute-start = (f32[32,1,512]{2,1,0:T(1,128)S(1)}, f32[32,1,512]{2,1,0:T(1,128)S(1)}, u32[]{:S(2)}, u32[]{:S(2)}) collective-permute-start(f32[32,1,512]{2,1,0:T(1,128)S(1)} %get-tuple-element.151), channel_id=1, source_target_pairs={{2,0},{4,2},{6,4},{8,6},{10,8},{12,10},{14,12},{16,14},{18,16},{20... | collective-permute-start | bytes 196616 | tf_op jit(solution)/shard_map/while/body/ppermute | solution.py:28
  397.9 7.5 %collective-permute-start = (f32[32,1,512]{2,1,0:T(1,128)S(1)}, f32[32,1,512]{2,1,0:T(1,128)S(1)}, u32[]{:S(2)}, u32[]{:S(2)}) collective-permute-start(f32[32,1,512]{2,1,0:T(1,128)S(1)} %get-tuple-element.151), channel_id=1, source_target_pairs={{2,0},{4,2},{6,4},{8,6},{10,8},{12,10},{14,12},{16,14},{18,16},{20... | collective-permute-start | bytes 196616 | tf_op jit(solution)/shard_map/while/body/ppermute | solution.py:28
  412.1 7.5 %collective-permute-start = (f32[32,1,512]{2,1,0:T(1,128)S(1)}, f32[32,1,512]{2,1,0:T(1,128)S(1)}, u32[]{:S(2)}, u32[]{:S(2)}) collective-permute-start(f32[32,1,512]{2,1,0:T(1,128)S(1)} %get-tuple-element.151), channel_id=1, source_target_pairs={{2,0},{4,2},{6,4},{8,6},{10,8},{12,10},{14,12},{16,14},{18,16},{20... | collective-permute-start | bytes 196616 | tf_op jit(solution)/shard_map/while/body/ppermute | solution.py:28
  426.2 7.5 %collective-permute-start = (f32[32,1,512]{2,1,0:T(1,128)S(1)}, f32[32,1,512]{2,1,0:T(1,128)S(1)}, u32[]{:S(2)}, u32[]{:S(2)}) collective-permute-start(f32[32,1,512]{2,1,0:T(1,128)S(1)} %get-tuple-element.151), channel_id=1, source_target_pairs={{2,0},{4,2},{6,4},{8,6},{10,8},{12,10},{14,12},{16,14},{18,16},{20... | collective-permute-start | bytes 196616 | tf_op jit(solution)/shard_map/while/body/ppermute | solution.py:28
  440.4 7.5 %collective-permute-start = (f32[32,1,512]{2,1,0:T(1,128)S(1)}, f32[32,1,512]{2,1,0:T(1,128)S(1)}, u32[]{:S(2)}, u32[]{:S(2)}) collective-permute-start(f32[32,1,512]{2,1,0:T(1,128)S(1)} %get-tuple-element.151), channel_id=1, source_target_pairs={{2,0},{4,2},{6,4},{8,6},{10,8},{12,10},{14,12},{16,14},{18,16},{20... | collective-permute-start | bytes 196616 | tf_op jit(solution)/shard_map/while/body/ppermute | solution.py:28
  454.6 7.5 %collective-permute-start = (f32[32,1,512]{2,1,0:T(1,128)S(1)}, f32[32,1,512]{2,1,0:T(1,128)S(1)}, u32[]{:S(2)}, u32[]{:S(2)}) collective-permute-start(f32[32,1,512]{2,1,0:T(1,128)S(1)} %get-tuple-element.151), channel_id=1, source_target_pairs={{2,0},{4,2},{6,4},{8,6},{10,8},{12,10},{14,12},{16,14},{18,16},{20... | collective-permute-start | bytes 196616 | tf_op jit(solution)/shard_map/while/body/ppermute | solution.py:28
  474.6 7.2 %all-to-all-start = ((f32[32,2,128]{2,0,1:T(8,128)}), f32[32,2,128]{2,0,1:T(8,128)S(1)}, u32[]{:S(2)}, u32[]{:S(2)}) async-start(f32[32,2,128]{2,0,1:T(8,128)} %broadcast_select_fusion), calls=%async_computation | async-start | bytes 65536 | tf_op jit(solution)/shard_map/all_to_all | solution.py:89
  (44 other events, 298.3 us)
Sparse Core Ops, SparseCore 0:
  9.5 35.8 all-gather.1
